TPU v7x, 32 devices: a whole 2x2x4 slice. The times are simulated.
32 devices in a mesh: groups: 2 (over y), cand: 4 (over z), tensor: 4 (over x, core).
Axes of the slice: x: 2, y: 2, z: 4, core: 2. Of those that a mesh axis runs over, the one named last changes fastest.
Arguments:
- response_latest_embeddings: bfloat16 [16, 384, 8192], P(('groups', 'cand'), None, 'tensor'), parts along dimension 0, may hold values from -6 to 6
- critic_probe_projector: bfloat16 [8192, 4096], P('cand', 'tensor'), may hold values from -0.0625 to 0.0625
- critic_pair_projector: bfloat16 [8192, 2048], P('cand', 'tensor'), may hold values from -0.0625 to 0.0625
- critic_stored_pairs: bfloat16 [16, 2048, 2048], P(('groups', 'cand'), None, 'tensor'), parts along dimension 0, may hold values from -1000 to 1000
- critic_grading_vector: float32 [4096], P('tensor'), may hold values from -6 to 6
- actor_stored_pairs: bfloat16 [16, 2048, 8, 256], P(('groups', 'cand'), None, 'tensor'), parts along dimension 0, may hold values from -1000 to 1000
- filled_extents: int32 [16], P('groups'), parts along dimension 0, may hold values from 1 to 2048, as said below
- kept_responses: int32 [8], P('groups'), parts along dimension 0, may hold values from 0 to 7, as said below
- actor_latest_probes: bfloat16 [8, 4, 4096], P(('groups', 'cand'), None, 'tensor'), parts along dimension 0, may hold values from -6 to 6
- actor_latest_pairs: bfloat16 [8, 4, 2048], P(('groups', 'cand'), None, 'tensor'), parts along dimension 0, may hold values from -6 to 6
Outputs:
- token_rewards: float32 [16, 384], P(('groups', 'cand')), parts along dimension 0
- actor_mixing_result: bfloat16 [8, 4, 4096], P(('groups', 'cand'), None, 'tensor'), parts along dimension 0
There are 2 independent parts, one for each index of `groups`. A program takes and returns all parts, laid end to end along the dimension named above; an argument that names none is the same for every part. Nothing has to cross between parts.
Inputs may be any that keep to these rules, and one draw needn't show every extreme that they name: `kept_responses`: distinct candidate ids, always including 0 and 7. `filled_extents`: some candidate has exactly 2048 live tokens.
All inputs are finite; a program needn't handle non-finite values.
Results may differ from a plain program's by a relative error of at most 0.012.
The roundings to bfloat16 on the way count: a program that leaves them out, or rounds other values in their place, can miss the bound.
Values may be sent and summed in bfloat16 or wider, within the bound.
A program may use at most 128 MiB of HBM per device.

v0:
```python
import functools

import jax
import jax.numpy as jnp
from jax import lax
from jax.experimental import pallas as pl
from jax.experimental.pallas import tpu as pltpu
from jax.sharding import PartitionSpec as P

HD = 128
CW = 2 * HD
AHEAD = 2
MESH = pl.DeviceIdType.MESH

masked_value = -1e30


def project_kernel(
    nz, nt, per_group,
    x_ref, wq_ref, wkv_ref, cache_ref, grade_ref, slots_ref, out_ref, mine_ref,
    xbuf, wbuf, cbuf, acts,
    load_sem, right_sem, left_sem, line_sem, pair_send, pair_recv,
    x_right, x_left, x_line, x_pair_send, x_pair_recv,
    given, give_send, give_recv,
):
    nchunk, depth, _ = wbuf.shape
    dz = depth // nz
    half = dz // 2
    nx = nt // 2
    cands, span, _ = out_ref.shape
    context = cbuf.shape[1]
    qchunks = per_group * HD // CW
    stride = 1 + qchunks
    y = lax.axis_index("groups")
    z = lax.axis_index("cand")
    t = lax.axis_index("tensor")
    x = t // 2
    c = t - 2 * x

    loads = []
    for k in range(nchunk):
        g, j = k // stride, k % stride
        if j == 0:
            src = wkv_ref.at[:, pl.ds(g * CW, CW)]
        else:
            src = wq_ref.at[:, pl.ds((g * qchunks + j - 1) * CW, CW)]
        loads.append(
            pltpu.make_async_copy(
                src, wbuf.at[k, pl.ds(pl.multiple_of(z * dz, dz), dz), :], load_sem.at[k]
            )
        )
    x_load = pltpu.make_async_copy(x_ref, xbuf.at[t], load_sem.at[nchunk])
    c_load = pltpu.make_async_copy(cache_ref, cbuf, load_sem.at[nchunk + 1])
    for k in range(min(AHEAD, nchunk)):
        loads[k].start()
    x_load.start()
    for k in range(min(AHEAD, nchunk), nchunk):
        loads[k].start()
    c_load.start()

    barrier = pltpu.get_barrier_semaphore()

    def greet(device):
        pl.semaphore_signal(barrier, inc=1, device_id=device, device_id_type=MESH)

    greet({"groups": 1 - y})
    greet({"tensor": 2 * x + 1 - c})

    def greet_peer(d, carry):
        greet({"cand": lax.rem(z + d, nz)})
        return carry

    lax.fori_loop(1, nz, greet_peer, 0)

    @pl.when(x > 0)
    def _():
        greet({"tensor": t - 2})

    @pl.when(x < nx - 1)
    def _():
        greet({"tensor": t + 2})

    ends = [x > 0, x < nx - 1]
    pl.semaphore_wait(barrier, nz + 1 + sum(e.astype(jnp.int32) for e in ends))

    def remote(ref, send, recv, device):
        return pltpu.make_async_remote_copy(
            src_ref=ref, dst_ref=ref, send_sem=send, recv_sem=recv,
            device_id=device, device_id_type=MESH,
        )

    def piece(k, o, side):
        return wbuf.at[k, pl.ds(pl.multiple_of(o * dz + side * half, half), half), :]

    def go_right(k, o):
        return remote(piece(k, o, y), right_sem.at[k, o], line_sem.at[k, o], {"cand": z + 1})

    def go_left(k, o):
        return remote(piece(k, o, y), left_sem.at[k, o], line_sem.at[k, o], {"cand": z - 1})

    def to_pair(k, o):
        return remote(piece(k, o, y), pair_send.at[k, o], pair_recv.at[k, o], {"groups": 1 - y})

    def from_pair(k, o):
        return remote(piece(k, o, 1 - y), pair_send.at[k, o], pair_recv.at[k, o], {"groups": 1 - y})

    def send_own(k):
        @pl.when(z < nz - 1)
        def _():
            go_right(k, z).start()

        @pl.when(z > 0)
        def _():
            go_left(k, z).start()

    def give(o):
        return pltpu.make_async_remote_copy(
            src_ref=slots_ref.at[o], dst_ref=given.at[z], send_sem=give_send.at[o],
            recv_sem=give_recv.at[z], device_id={"cand": o}, device_id_type=MESH,
        )

    def get(o):
        return pltpu.make_async_remote_copy(
            src_ref=slots_ref.at[o], dst_ref=given.at[o], send_sem=give_send.at[o],
            recv_sem=give_recv.at[o], device_id={"cand": o}, device_id_type=MESH,
        )

    def x_go_right(o):
        return remote(xbuf.at[2 * o + c], x_right.at[o], x_line.at[o], {"tensor": t + 2})

    def x_go_left(o):
        return remote(xbuf.at[2 * o + c], x_left.at[o], x_line.at[o], {"tensor": t - 2})

    def x_to_pair(o):
        return remote(xbuf.at[2 * o + c], x_pair_send.at[o], x_pair_recv.at[o], {"tensor": 2 * x + 1 - c})

    def x_from_pair(o):
        return remote(xbuf.at[2 * o + 1 - c], x_pair_send.at[o], x_pair_recv.at[o], {"tensor": 2 * x + 1 - c})

    def give_one(d, carry):
        give(lax.rem(z + d, nz)).start()
        return carry

    lax.fori_loop(1, nz, give_one, 0)
    for k in range(min(AHEAD, nchunk)):
        loads[k].wait()
        send_own(k)
    x_load.wait()

    @pl.when(x < nx - 1)
    def _():
        x_go_right(x).start()

    @pl.when(x > 0)
    def _():
        x_go_left(x).start()

    x_to_pair(x).start()
    for k in range(min(AHEAD, nchunk), nchunk):
        loads[k].wait()
    c_load.wait()
    out_ref[...] = jnp.zeros_like(out_ref)

    def finish_x():
        for d in range(1, nx):
            @pl.when(x - d >= 0)
            def _(d=d):
                x_go_right(x - d).wait_recv()
                x_to_pair(x - d).start()

                @pl.when(x < nx - 1)
                def _():
                    x_go_right(x - d).start()

            @pl.when(x + d < nx)
            def _(d=d):
                x_go_left(x + d).wait_recv()
                x_to_pair(x + d).start()

                @pl.when(x > 0)
                def _():
                    x_go_left(x + d).start()

        for o in range(nx):
            x_from_pair(o).wait_recv()

    def relay(k, first, last):
        def one(d, carry):
            @pl.when(z - d >= 0)
            def _():
                o = z - d
                go_right(k, o).wait_recv()

                @pl.when(z < nz - 1)
                def _():
                    go_right(k, o).start()

                to_pair(k, o).start()

            @pl.when(z + d < nz)
            def _():
                o = z + d
                go_left(k, o).wait_recv()

                @pl.when(z > 0)
                def _():
                    go_left(k, o).start()

                to_pair(k, o).start()

            return carry

        lax.fori_loop(first, last, one, 0)

    rows = cands * span
    dx = depth // nt
    row_tile = rows // 3

    def attend(k):
        g = k // stride
        base = pl.multiple_of(g * CW, CW)
        kv_at = g * stride
        ri = lax.broadcasted_iota(jnp.int32, (span, span), 0)
        ci = lax.broadcasted_iota(jnp.int32, (span, span), 1)
        head0 = (g * qchunks + (k - kv_at) - 1) * 2

        def one(b, carry):
            at = pl.ds(pl.multiple_of(b * span, span), span)
            old_k = cbuf[b, :, pl.ds(base, HD)]
            old_v = cbuf[b, :, pl.ds(pl.multiple_of(base + HD, HD), HD)]
            new_k = acts[kv_at, at, :HD]
            new_v = acts[kv_at, at, HD:]
            for h in range(2):
                q = acts[k, at, h * HD:(h + 1) * HD]
                dims = (((1,), (1,)), ((), ()))
                s1 = lax.dot_general(q, old_k, dims, preferred_element_type=jnp.float32)
                s2 = lax.dot_general(q, new_k, dims, preferred_element_type=jnp.float32)
                s2 = jnp.where(ri >= ci, s2, masked_value)
                top = jnp.maximum(
                    jnp.max(s1, axis=1, keepdims=True), jnp.max(s2, axis=1, keepdims=True)
                )
                scale = HD ** -0.5
                e1 = jnp.exp((s1 - top) * scale)
                e2 = jnp.exp((s2 - top) * scale)
                total = jnp.sum(e1, axis=1, keepdims=True) + jnp.sum(e2, axis=1, keepdims=True)
                o = jnp.dot(e1.astype(jnp.bfloat16), old_v, preferred_element_type=jnp.float32)
                o = o + jnp.dot(e2.astype(jnp.bfloat16), new_v, preferred_element_type=jnp.float32)
                weight = grade_ref[pl.ds(head0 + h, 1), :]
                out_ref[b] += (o / total) * weight
            return carry

        lax.fori_loop(0, cands, one, 0)

    def project(k):
        def take(d, carry):
            o = jnp.where(d < z, d, d + 1)
            from_pair(k, o).wait_recv()
            return carry

        lax.fori_loop(0, nz - 1, take, 0)

        def tile(r, carry):
            at = pl.ds(pl.multiple_of(r * row_tile, row_tile), row_tile)
            acc = jnp.zeros((row_tile, CW), jnp.float32)
            for s in range(nt):
                acc = acc + jnp.dot(
                    xbuf[s, at, :], wbuf[k, s * dx:(s + 1) * dx, :],
                    preferred_element_type=jnp.float32,
                )
            acts[k, at, :] = acc.astype(jnp.bfloat16)
            return carry

        lax.fori_loop(0, rows // row_tile, tile, 0)

    def units(first, last, unit):
        def one(j, carry):
            unit(j)
            return carry

        lax.fori_loop(first, last, one, 0)

    def attend_if(k):
        @pl.when(lax.rem(k, stride) != 0)
        def _():
            attend(k)

    def step(k, carry):
        @pl.when(k + AHEAD < nchunk)
        def _():
            send_own(k + AHEAD)

        relay(k, 1, 2)

        @pl.when(k == 2)
        def _():
            finish_x()

        @pl.when(k >= 2)
        def _():
            project(jnp.where(k == 2, 0, k - 1))

        relay(k, 2, min(3, nz))

        @pl.when(k == 2)
        def _():
            project(k - 1)

        @pl.when(k >= 2)
        def _():
            attend_if(k - 1)

        relay(k, 3, nz)
        return carry

    lax.fori_loop(0, nchunk, step, 0)
    units(nchunk - 1, nchunk, project)
    units(nchunk - 1, nchunk, attend_if)
    mine_ref[...] = slots_ref[z].astype(jnp.float32)

    def get_one(d, carry):
        o = lax.rem(z + d, nz)
        get(o).wait_recv()
        mine_ref[...] += given[o].astype(jnp.float32)
        give(o).wait_send()
        return carry

    lax.fori_loop(1, nz, get_one, 0)

    def drain(k, carry):
        def one(o, c2):
            @pl.when((o <= z) & (z < nz - 1))
            def _():
                go_right(k, o).wait_send()

            @pl.when((o >= z) & (z > 0))
            def _():
                go_left(k, o).wait_send()

            @pl.when(o != z)
            def _():
                to_pair(k, o).wait_send()

            return c2

        lax.fori_loop(0, nz, one, 0)
        return carry

    lax.fori_loop(0, nchunk, drain, 0)
    for o in range(nx):
        x_to_pair(o).wait_send()

        @pl.when((o <= x) & (x < nx - 1))
        def _(o=o):
            x_go_right(o).wait_send()

        @pl.when((o >= x) & (x > 0))
        def _(o=o):
            x_go_left(o).wait_send()


def reward_partial(nz, nt, x, wq, wkv, cache, grade, slots):
    cands, span, dx = x.shape
    rows = cands * span
    depth = wq.shape[0] * nz
    groups_here = wkv.shape[1] // CW
    per_group = wq.shape[1] // HD // groups_here
    nchunk = (wq.shape[1] + wkv.shape[1]) // CW
    dma = pltpu.SemaphoreType.DMA
    nx = nt // 2
    anywhere = pl.BlockSpec(memory_space=pl.ANY)
    return pl.pallas_call(
        functools.partial(project_kernel, nz, nt, per_group),
        out_shape=(
            jax.ShapeDtypeStruct((cands, span, HD), jnp.float32),
            jax.ShapeDtypeStruct(slots.shape[1:], jnp.float32),
        ),
        in_specs=[anywhere] * 4 + [pl.BlockSpec(memory_space=pltpu.VMEM)] * 2,
        out_specs=(pl.BlockSpec(memory_space=pltpu.VMEM),) * 2,
        scratch_shapes=[
            pltpu.VMEM((nt, rows, dx), jnp.bfloat16),
            pltpu.VMEM((nchunk, depth, CW), jnp.bfloat16),
            pltpu.VMEM(cache.shape, jnp.bfloat16),
            pltpu.VMEM((nchunk, rows, CW), jnp.bfloat16),
            dma((nchunk + 2,)),
            dma((nchunk, nz)), dma((nchunk, nz)), dma((nchunk, nz)),
            dma((nchunk, nz)), dma((nchunk, nz)),
            dma((nx,)), dma((nx,)), dma((nx,)), dma((nx,)), dma((nx,)),
            pltpu.VMEM(slots.shape, jnp.bfloat16), dma((nz,)), dma((nz,)),
        ],
        compiler_params=pltpu.CompilerParams(
            collective_id=0, has_side_effects=True, vmem_limit_bytes=67043328
        ),
    )(x.reshape(rows, dx), wq, wkv, cache, grade.reshape(-1, HD), slots)


def gather_kernel(nz, own_ref, out_ref, buf, send, recv):
    z = lax.axis_index("cand")
    barrier = pltpu.get_barrier_semaphore()

    def greet(d, carry):
        pl.semaphore_signal(
            barrier, inc=1, device_id={"cand": lax.rem(z + d, nz)}, device_id_type=MESH
        )
        return carry

    lax.fori_loop(1, nz, greet, 0)
    pl.semaphore_wait(barrier, nz - 1)

    def copy(o, lands):
        return pltpu.make_async_remote_copy(
            src_ref=own_ref, dst_ref=buf.at[lands], send_sem=send.at[o],
            recv_sem=recv.at[lands], device_id={"cand": o}, device_id_type=MESH,
        )

    def start(d, carry):
        copy(lax.rem(z + d, nz), z).start()
        return carry

    lax.fori_loop(1, nz, start, 0)
    out_ref[z] = own_ref[...]

    def finish(d, carry):
        o = lax.rem(z + d, nz)
        copy(o, o).wait_recv()
        out_ref[o] = buf[o]
        copy(o, z).wait_send()
        return carry

    lax.fori_loop(1, nz, finish, 0)


def gather_slots(nz, own):
    lanes, count, width = own.shape
    flat = own.reshape(lanes * count, width)
    vmem = pl.BlockSpec(memory_space=pltpu.VMEM)
    whole = pl.pallas_call(
        functools.partial(gather_kernel, nz),
        out_shape=jax.ShapeDtypeStruct((nz,) + flat.shape, own.dtype),
        in_specs=[vmem],
        out_specs=vmem,
        scratch_shapes=[
            pltpu.VMEM((nz,) + flat.shape, own.dtype),
            pltpu.SemaphoreType.DMA((nz,)), pltpu.SemaphoreType.DMA((nz,)),
        ],
        compiler_params=pltpu.CompilerParams(
            collective_id=1, has_side_effects=True, vmem_limit_bytes=1 << 22
        ),
    )(flat)
    return whole.reshape(nz * lanes, count, width)


def policy(
    nz, cand_here, actor_stored_pairs, filled_extents, kept_responses, actor_latest_probes, actor_latest_pairs
):
    key_scale = HD ** (-0.5)
    device_here = lax.axis_index("cand")
    lane_number = kept_responses.shape[0]
    new_count = actor_latest_probes.shape[1]
    kv_here = actor_stored_pairs.shape[2]
    policy_heads = actor_latest_probes.shape[2] // HD
    policy_group = policy_heads // kv_here
    cache_len = actor_stored_pairs.shape[1]
    causal_new = lax.broadcasted_iota(jnp.int32, (new_count, new_count), 0) >= lax.broadcasted_iota(
        jnp.int32, (new_count, new_count), 1
    )
    both = gather_slots(
        nz, jnp.concatenate([actor_latest_probes, actor_latest_pairs], axis=2)
    )
    all_queries = both[..., : policy_heads * HD]
    all_fresh = both[..., policy_heads * HD:]
    ids_here = device_here * cand_here + lax.broadcasted_iota(jnp.int32, (cand_here,), 0)
    matched = kept_responses[None, :] == ids_here[:, None]
    slot_index = jnp.sum(
        jnp.where(matched, lax.broadcasted_iota(jnp.int32, (cand_here, lane_number), 1), 0), axis=1
    )
    own_queries = jnp.take(all_queries, slot_index, axis=0).reshape(
        cand_here, new_count, kv_here, policy_group, HD
    )
    own_fresh = jnp.take(all_fresh, slot_index, axis=0).reshape(
        cand_here, new_count, kv_here, 2 * HD
    )
    sequence_places = lax.broadcasted_iota(jnp.int32, (cache_len,), 0)
    living = sequence_places[None, :] < jnp.take(filled_extents, ids_here)[:, None]
    living = living[:, None, None, None, :]
    scores = (
        jnp.einsum(
            "cikgd,ctkd->ckgit", own_queries, actor_stored_pairs[..., :HD],
            preferred_element_type=jnp.float32,
        )
        * key_scale
    )
    scores = jnp.where(living, scores, masked_value)
    fresh_scores = (
        jnp.einsum(
            "cikgd,cjkd->ckgij", own_queries, own_fresh[..., :HD], preferred_element_type=jnp.float32
        )
        * key_scale
    )
    fresh_scores = jnp.where(causal_new, fresh_scores, masked_value)
    peak = jnp.maximum(jnp.max(scores, axis=-1), jnp.max(fresh_scores, axis=-1))
    old_weights = jnp.where(living, jnp.exp(scores - peak[..., None]), 0.0)
    fresh_weights = jnp.where(causal_new, jnp.exp(fresh_scores - peak[..., None]), 0.0)
    denominator = jnp.sum(old_weights, axis=-1) + jnp.sum(fresh_weights, axis=-1)
    numerator = jnp.einsum(
        "ckgit,ctkd->ckgid", old_weights, actor_stored_pairs[..., HD:],
        preferred_element_type=jnp.float32,
    )
    numerator = numerator + jnp.einsum(
        "ckgij,cjkd->ckgid", fresh_weights, own_fresh[..., HD:], preferred_element_type=jnp.float32
    )
    result = numerator / denominator[..., None]
    flattened = jnp.transpose(result, (0, 3, 1, 2, 4)).reshape(
        cand_here, new_count * policy_heads * HD
    )
    placed = jnp.einsum(
        "cs,cx->sx", matched.astype(jnp.float32), flattened, precision=lax.Precision.HIGHEST
    )
    return placed.reshape(nz, lane_number // nz * new_count, policy_heads * HD).astype(jnp.bfloat16)


def local(
    nz, nt,
    response_latest_embeddings,
    critic_probe_projector,
    critic_pair_projector,
    critic_stored_pairs,
    critic_grading_vector,
    actor_stored_pairs,
    filled_extents,
    kept_responses,
    actor_latest_probes,
    actor_latest_pairs,
):
    slots = policy(
        nz, response_latest_embeddings.shape[0], actor_stored_pairs, filled_extents, kept_responses,
        actor_latest_probes, actor_latest_pairs,
    )
    shares, mine = reward_partial(
        nz, nt, response_latest_embeddings, critic_probe_projector, critic_pair_projector,
        critic_stored_pairs, critic_grading_vector, slots,
    )
    token_rewards = lax.psum(jnp.sum(shares, axis=-1), "tensor")
    slot_rows = mine.reshape(actor_latest_probes.shape).astype(jnp.bfloat16)
    return (token_rewards, slot_rows)


def solution(mesh):
    placed = (
        P(("groups", "cand"), None, "tensor"),
        P("cand", "tensor"),
        P("cand", "tensor"),
        P(("groups", "cand"), None, "tensor"),
        P("tensor"),
        P(("groups", "cand"), None, "tensor", None),
        P("groups"),
        P("groups"),
        P(("groups", "cand"), None, "tensor"),
        P(("groups", "cand"), None, "tensor"),
    )
    return jax.shard_map(
        functools.partial(local, mesh.shape["cand"], mesh.shape["tensor"]),
        mesh=mesh,
        in_specs=placed,
        out_specs=(P(("groups", "cand"), None), P(("groups", "cand"), None, "tensor")),
        check_vma=False,
    )
```

profile of v0, /device:TPU:0, one launch (start us, length us, event | category | flops | bytes accessed | tf_op | source)
XLA Modules:
  0.0 284.4 jit_solution(992208703682408601)
XLA Ops:
  0.7 1.3 gather_fusion
  2.0 0.8 fusion.16
  2.8 0.1 iota_compare_fusion
  2.9 0.7 maximum_bitcast_fusion.own_ref
  3.7 7.6 %shard_map.113 = bf16[4,4,1536]{2,1,0:T(4,128)(2,1)S(1)} custom-call(bf16[4,1536]{1,0:T(4,128)(2,1)S(1)} %maximum_bitcast_fusion.own_ref), custom_call_target="tpu_custom_call" | custom-call | tf_op jit(solution)/shard_map/pallas_call | solution.py:436
  11.3 0.6 gather_fusion.1
  11.9 0.6 gather_fusion.2
  12.4 0.1 broadcast_select_fusion
  12.5 0.3 fusion.25
  12.9 4.7 %fusion.23 = (bf16[2,2048,2,128]{3,2,1,0:T(2,128)(2,1)S(1)}, bf16[2,2048,2,128]{3,2,1,0:T(2,128)(2,1)S(1)}) fusion(bf16[2,2048,2,256]{3,2,1,0:T(2,128)(2,1)} %param.15), kind=kLoop, calls=%fused_computation.54 | loop fusion | bytes 8388608 | tf_op jit(solution)/shard_map/slice | solution.py:487
  17.6 0.8 fusion.24
  18.4 0.0 copy-start
  18.4 0.6 fusion.2
  19.0 0.4 fusion.7
  19.4 0.1 fusion.11
  19.5 0.3 fusion.4
  19.9 0.0 copy-done
  19.9 0.3 fusion.15
  20.2 0.6 copy.57.slots_ref
  20.8 254.9 %shard_map.114 = (f32[2,384,128]{2,1,0:T(8,128)}, f32[4,1024]{1,0:T(4,128)}) custom-call(bf16[768,2048]{1,0:T(8,128)(2,1)} %bitcast.56, bf16[2048,1024]{1,0:T(8,128)(2,1)} %wq_ref.1, bf16[2048,512]{1,0:T(8,128)(2,1)} %wkv_ref.1, bf16[2,2048,512]{2,1,0:T(8,128)(2,1)} %cache_ref.1, f32[8,128]{1,0:T(8,128)} %bitcast.59, bf16[4,4,1024]{2,1,0:T(4,128)(2,1)} %copy.57.slots_ref), custom_call_target="tpu_custom_call" | custom-call | tf_op jit(solution)/shard_map/pallas_call | solution.py:371
  275.7 1.2 reduce_sum.42
  276.9 6.2 %psum.7 = f32[2,384]{1,0:T(2,128)} all-reduce(f32[2,384]{1,0:T(2,128)S(1)} %reduce_sum.42), channel_id=1, replica_groups=mesh['groups'=2,'cand'=4,'tensor'=4] {'tensor'}, use_global_device_ids=true, to_apply=%region_6.7 | all-reduce | flops 768 | bytes 6144 | tf_op jit(solution)/shard_map/psum | solution.py:542
  283.1 1.3 convert_bitcast_fusion
  (14 shorter events, 0.1 us)
Async XLA Ops:
  18.4 1.5 copy-start
where the time goes:
time: 285 us; the launch traced here: 284 us
  Pallas kernels  262 us (92%)
  local copies, waits for them, and re-layouts  7.83 us (3%)
  blocking collectives  6.24 us (2%)
  other arithmetic  4.77 us (2%)
    pallas_call x1, Pallas kernels, reward_partial(): pl.pallas_call(functools.partial(project_kernel, nz, nt, per_group), out_...  255 us
    pallas_call x1, Pallas kernels, gather_slots(): pl.pallas_call(functools.partial(gather_kernel, nz), out_shape=jax.ShapeD...  7.58 us
    psum x1, blocking collectives, local(): token_rewards = lax.psum(jnp.sum(shares, axis=-1), 'tensor')  6.24 us

commit v1 on v0

v1 whole, which is shorter than its diff:
```python
import functools

import jax
import jax.numpy as jnp
from jax import lax
from jax.experimental import pallas as pl
from jax.experimental.pallas import tpu as pltpu
from jax.sharding import PartitionSpec as P

HD = 128
CW = 2 * HD
SPLIT = 2
AHEAD = 4
LAG = 4
TILES = 4
MESH = pl.DeviceIdType.MESH

masked_value = -1e30
LOG2E = 1.4426950408889634


def when(cond, body):
    pl.when(cond)(body)


def reward_kernel(
    nz, nt, per_group,
    x_ref, wq_ref, wkv_ref, cache_ref, pcache_ref,
    grade_ref, probes_ref, pairs_ref, kept_ref, extents_ref,
    reward_ref, mix_ref,
    xbuf, sbuf, wbuf, cbuf, pbuf, acts, sres, part, toks,
    qall, pall, qsel, psel, qrow, krow, vrow, placed, given, mine,
    load_sem, right_sem, left_sem, line_sem, pair_send, pair_recv,
    x_right, x_left, x_line, x_psend, x_precv,
    s_send, s_recv, sx_right, sx_left, sx_line, sx_psend, sx_precv,
    r_send, r_recv, t_send, t_recv,
    q_send, q_recv, p_send, p_recv, give_send, give_recv,
):
    nchunk, depth, _ = wbuf.shape
    nv = nchunk * SPLIT
    dz = depth // nz
    sub = dz // SPLIT
    nx = nt // 2
    cands, span, _ = part.shape
    rows = cands * span
    dx = depth // nt
    qchunks = per_group * HD // CW
    groups = nchunk // (1 + qchunks)
    qrows = rows // TILES
    per_cand = TILES // cands
    srows = rows // nv
    vx = max(2, nv // 4 * 2)
    sx = vx - 1
    sp_step = []
    for i in range(TILES):
        at = nv if i == TILES - 1 else max(nv - TILES + 1 + i, 4 * groups + 1)
        sp_step.append(at if at < nv else nv)
    off_step = [s + 1 if s + 1 < nv else nv + 1 for s in sp_step]

    def whole16(n):
        return max(sub // 2, int(round(n / 16)) * 16)

    share_first = whole16(sub * 2 / 3)
    share_mid = whole16(sub * 7 / 12)
    share_last = sub // 2

    y = lax.axis_index("groups")
    z = lax.axis_index("cand")
    t = lax.axis_index("tensor")
    x = t // 2
    c = t - 2 * x
    at_end = (z == 0) | (z == nz - 1)
    beside = (z == 1) | (z == nz - 2)
    inner = jnp.where(z == 0, 1, nz - 2)
    outer = jnp.where(z == 1, 0, nz - 1)

    def is_away(p):
        return (p < 2 * groups) & (lax.rem(p, 2) == 1)

    def is_query(p):
        return (p >= 2 * groups) | (lax.rem(p, 2) == 1)

    def columns(p):
        if p < 2 * groups:
            g, j = p // 2, (p % 2) * qchunks
        else:
            g, j = divmod(p - 2 * groups, qchunks - 1)
            j += 1
        if j == 0:
            return wkv_ref.at[:, pl.ds(g * CW, CW)]
        return wq_ref.at[:, pl.ds((g * qchunks + j - 1) * CW, CW)]

    own_rows = pl.ds(pl.multiple_of(z * dz, dz), dz)
    loads = [
        pltpu.make_async_copy(columns(p), wbuf.at[p, own_rows, :], load_sem.at[p])
        for p in range(nchunk)
    ]
    x_load = pltpu.make_async_copy(x_ref, xbuf.at[t], load_sem.at[nchunk])
    c_load = pltpu.make_async_copy(cache_ref, cbuf, load_sem.at[nchunk + 1])
    p_loads = [
        pltpu.make_async_copy(pcache_ref.at[b], pbuf, load_sem.at[nchunk + 2 + b])
        for b in range(cands)
    ]
    loads[0].start()
    x_load.start()
    for p in range(1, nchunk):
        loads[p].start()
    p_loads[0].start()
    c_load.start()

    barrier = pltpu.get_barrier_semaphore()

    def greet(device):
        pl.semaphore_signal(barrier, inc=1, device_id=device, device_id_type=MESH)

    greet({"groups": 1 - y})

    def greet_cand(d, carry):
        greet({"cand": lax.rem(z + d, nz)})
        return carry

    def greet_tensor(d, carry):
        greet({"tensor": lax.rem(t + d, nt)})
        return carry

    lax.fori_loop(1, nz, greet_cand, 0)
    lax.fori_loop(1, nt, greet_tensor, 0)
    pl.semaphore_wait(barrier, nz + nt - 1)

    def remote(src, dst, send, recv, device):
        return pltpu.make_async_remote_copy(
            src_ref=src, dst_ref=dst, send_sem=send, recv_sem=recv,
            device_id=device, device_id_type=MESH,
        )

    def hop(src, dst, body):
        first = (src == 0) | (src == nz - 1)
        last = (dst == 0) | (dst == nz - 1)
        when(first, lambda: body(share_first))
        when(last, lambda: body(share_last))
        when(jnp.logical_not(first | last), lambda: body(share_mid))

    def piece(v, o, start, size):
        p = v // SPLIT
        base = o * dz + (v - p * SPLIT) * sub + start
        return wbuf.at[p, pl.ds(pl.multiple_of(base, 16), size), :]

    def go_right(v, o, s):
        ref = piece(v, o, y * (sub - s), s)
        return remote(ref, ref, right_sem.at[v, o], line_sem.at[v, o], {"cand": z + 1})

    def go_left(v, o, s):
        ref = piece(v, o, y * (sub - s), s)
        return remote(ref, ref, left_sem.at[v, o], line_sem.at[v, o], {"cand": z - 1})

    def to_pair(v, o, s):
        ref = piece(v, o, y * s, sub - s)
        return remote(ref, ref, pair_send.at[v, o], pair_recv.at[v, o], {"groups": 1 - y})

    def from_pair(v, o, s):
        ref = piece(v, o, (1 - y) * s, sub - s)
        return remote(ref, ref, pair_send.at[v, o], pair_recv.at[v, o], {"groups": 1 - y})

    def sends_right(p):
        return (z < nz - 1) & jnp.logical_not(is_away(p) & (z + 1 == nz - 1))

    def sends_left(p):
        return (z > 0) & jnp.logical_not(is_away(p) & (z - 1 == 0))

    def send_own(v):
        p = v // SPLIT
        when(sends_right(p), lambda: hop(z, z + 1, lambda s: go_right(v, z, s).start()))
        when(sends_left(p), lambda: hop(z, z - 1, lambda s: go_left(v, z, s).start()))

    def relay(v, first, last):
        p = v // SPLIT
        here = jnp.logical_not(is_away(p) & at_end)

        def one(d, carry):
            @pl.when((z - d >= 0) & here)
            def _():
                o = z - d
                hop(z - 1, z, lambda s: go_right(v, o, s).wait_recv())
                when(sends_right(p), lambda: hop(z, z + 1, lambda s: go_right(v, o, s).start()))
                hop(z - 1, z, lambda s: to_pair(v, o, s).start())

            @pl.when((z + d < nz) & here)
            def _():
                o = z + d
                hop(z + 1, z, lambda s: go_left(v, o, s).wait_recv())
                when(sends_left(p), lambda: hop(z, z - 1, lambda s: go_left(v, o, s).start()))
                hop(z + 1, z, lambda s: to_pair(v, o, s).start())

            return carry

        lax.fori_loop(first, last, one, 0)

    def drain(v):
        p = v // SPLIT

        def one(o, carry):
            when(
                (o <= z) & sends_right(p),
                lambda: hop(z, z + 1, lambda s: go_right(v, o, s).wait_send()),
            )
            when(
                (o >= z) & sends_left(p),
                lambda: hop(z, z - 1, lambda s: go_left(v, o, s).wait_send()),
            )

            @pl.when((o != z) & jnp.logical_not(is_away(p) & at_end))
            def _():
                hop(jnp.where(o < z, z - 1, z + 1), z, lambda s: to_pair(v, o, s).wait_send())

            return carry

        lax.fori_loop(0, nz, one, 0)

    def row_gather(buf, at, right, left, line, psend, precv):
        def block(o, core):
            return buf.at[2 * o + core, at, :]

        def to_right(o):
            return remote(block(o, c), block(o, c), right(o), line(o), {"tensor": t + 2})

        def to_left(o):
            return remote(block(o, c), block(o, c), left(o), line(o), {"tensor": t - 2})

        def across(o, core):
            return remote(
                block(o, core), block(o, core), psend(o), precv(o), {"tensor": 2 * x + 1 - c}
            )

        def begin():
            when(x < nx - 1, lambda: to_right(x).start())
            when(x > 0, lambda: to_left(x).start())
            across(x, c).start()

        def finish():
            for d in range(1, nx):
                @pl.when(x - d >= 0)
                def _(d=d):
                    to_right(x - d).wait_recv()
                    when(x < nx - 1, lambda: to_right(x - d).start())
                    across(x - d, c).start()

                @pl.when(x + d < nx)
                def _(d=d):
                    to_left(x + d).wait_recv()
                    when(x > 0, lambda: to_left(x + d).start())
                    across(x + d, c).start()

            for o in range(nx):
                across(o, 1 - c).wait_recv()

        def settle():
            for o in range(nx):
                across(o, c).wait_send()
                when((o <= x) & (x < nx - 1), lambda o=o: to_right(o).wait_send())
                when((o >= x) & (x > 0), lambda o=o: to_left(o).wait_send())

        return begin, finish, settle

    x_begin, x_finish, x_settle = row_gather(
        xbuf, pl.ds(0, rows), lambda o: x_right.at[o], lambda o: x_left.at[o],
        lambda o: x_line.at[o], lambda o: x_psend.at[o], lambda o: x_precv.at[o],
    )

    def span_rows(j):
        return pl.ds(pl.multiple_of(j * srows, srows), srows)

    def lend(j):
        at = span_rows(j)
        return remote(
            xbuf.at[t, at, :], sbuf.at[t, at, :], s_send.at[j], s_recv.at[j], {"cand": inner}
        )

    def borrowed(j):
        return row_gather(
            sbuf, span_rows(j), lambda o: sx_right.at[j, o], lambda o: sx_left.at[j, o],
            lambda o: sx_line.at[j, o], lambda o: sx_psend.at[j, o], lambda o: sx_precv.at[j, o],
        )

    def tile_rows(i):
        return pl.ds(pl.multiple_of(i * qrows, qrows), qrows)

    def give_back(g, i):
        at = tile_rows(i)
        return remote(
            sres.at[g, at, :], acts.at[2 * g + 1, at, :], r_send.at[g, i], r_recv.at[g, i],
            {"cand": outer},
        )

    def get_back(g, i):
        at = acts.at[2 * g + 1, tile_rows(i), :]
        return remote(at, at, r_send.at[g, i], r_recv.at[g, i], {"cand": inner})

    def each(first, last, body):
        def one(j, carry):
            body(j)
            return carry

        lax.fori_loop(first, last, one, 0)

    def others(body):
        each(1, nz, lambda d: body(lax.rem(z + d, nz)))

    def ask(src, buf, send, recv, o, lands):
        return remote(src, buf.at[lands], send.at[o], recv.at[lands], {"cand": o})

    def ask_all(o):
        ask(probes_ref, qall, q_send, q_recv, o, z).start()
        ask(pairs_ref, pall, p_send, p_recv, o, z).start()

    others(ask_all)
    for v in range(AHEAD):
        if v % SPLIT == 0:
            loads[v // SPLIT].wait()
        send_own(v)
        if v == 0:
            x_load.wait()
            x_begin()
        when(at_end, lambda v=v: lend(v).start())
    for p in range(-(-AHEAD // SPLIT), nchunk):
        loads[p].wait()
    part[...] = jnp.zeros_like(part)

    lanes, fresh, _ = probes_ref.shape
    kv_here = pcache_ref.shape[2]
    tokens = pcache_ref.shape[1]
    pgroup = probes_ref.shape[2] // HD // kv_here
    prow = pgroup * fresh

    def match(o, l, b):
        same = kept_ref[o * lanes + l] == z * cands + b
        return jnp.where(same, 1.0, 0.0)

    def pick(o, q, kv, fresh_start):
        for b in range(cands):
            for l in range(lanes):
                m = match(o, l, b)
                if fresh_start and l == 0:
                    qsel[b] = q(l) * m
                    psel[b] = kv(l) * m
                else:
                    qsel[b] += q(l) * m
                    psel[b] += kv(l) * m

    def policy():
        pick(
            z, lambda l: probes_ref[l].astype(jnp.float32),
            lambda l: pairs_ref[l].astype(jnp.float32), True,
        )

        def take(o):
            ask(probes_ref, qall, q_send, q_recv, o, o).wait_recv()
            ask(pairs_ref, pall, p_send, p_recv, o, o).wait_recv()
            pick(
                o, lambda l: qall[o, l].astype(jnp.float32),
                lambda l: pall[o, l].astype(jnp.float32), False,
            )
            ask(probes_ref, qall, q_send, q_recv, o, z).wait_send()
            ask(pairs_ref, pall, p_send, p_recv, o, z).wait_send()

        others(take)
        for b in range(cands):
            for g in range(kv_here):
                for h in range(pgroup):
                    head = (g * pgroup + h) * HD
                    qrow[g * prow + h * fresh:g * prow + (h + 1) * fresh, :] = (
                        qsel[b, :, head:head + HD]
                    )
                krow[g * fresh:(g + 1) * fresh, :] = psel[b, :, g * CW:g * CW + HD]
                vrow[g * fresh:(g + 1) * fresh, :] = psel[b, :, g * CW + HD:(g + 1) * CW]
            p_loads[b].wait()
            old_k = pbuf[:, :, :HD].reshape(tokens * kv_here, HD)
            old_v = pbuf[:, :, HD:].reshape(tokens * kv_here, HD)
            q = qrow[...].astype(jnp.bfloat16)
            dims = (((1,), (1,)), ((), ()))
            s1 = lax.dot_general(q, old_k, dims, preferred_element_type=jnp.float32)
            s2 = lax.dot_general(
                q, krow[...].astype(jnp.bfloat16), dims, preferred_element_type=jnp.float32
            )
            r1 = lax.broadcasted_iota(jnp.int32, s1.shape, 0)
            c1 = lax.broadcasted_iota(jnp.int32, s1.shape, 1)
            r2 = lax.broadcasted_iota(jnp.int32, s2.shape, 0)
            c2 = lax.broadcasted_iota(jnp.int32, s2.shape, 1)
            live = extents_ref[z * cands + b]
            seen1 = (c1 % kv_here == r1 // prow) & (c1 < live * kv_here)
            seen2 = (c2 // fresh == r2 // prow) & (c2 % fresh <= r2 % fresh)
            s1 = jnp.where(seen1, s1, masked_value)
            s2 = jnp.where(seen2, s2, masked_value)
            top = jnp.maximum(
                jnp.max(s1, axis=1, keepdims=True), jnp.max(s2, axis=1, keepdims=True)
            )
            e1 = jnp.exp((s1 - top) * HD ** -0.5)
            e2 = jnp.exp((s2 - top) * HD ** -0.5)
            total = jnp.sum(e1, axis=1, keepdims=True) + jnp.sum(e2, axis=1, keepdims=True)
            out = jnp.dot(e1.astype(jnp.bfloat16), old_v, preferred_element_type=jnp.float32)
            out = out + jnp.dot(
                e2.astype(jnp.bfloat16), vrow[...].astype(jnp.bfloat16),
                preferred_element_type=jnp.float32,
            )
            if b + 1 < cands:
                p_loads[b + 1].start()
            out = out / total
            for o in range(nz):
                for l in range(lanes):
                    given_to = (out * match(o, l, b)).astype(jnp.bfloat16)
                    if b == 0:
                        placed[o, l] = given_to
                    else:
                        placed[o, l] += given_to

    def give(o):
        return remote(
            placed.at[o], given.at[z], give_send.at[o], give_recv.at[z], {"cand": o}
        )

    def get(o):
        return remote(
            placed.at[o], given.at[o], give_send.at[o], give_recv.at[o], {"cand": o}
        )

    def collect():
        mine[...] = placed[z].astype(jnp.float32)

        def add(o):
            get(o).wait_recv()
            mine[...] += given[o].astype(jnp.float32)
            give(o).wait_send()

        others(add)
        for l in range(lanes):
            for g in range(kv_here):
                for h in range(pgroup):
                    head = (g * pgroup + h) * HD
                    start = g * prow + h * fresh
                    mix_ref[l, :, head:head + HD] = (
                        mine[l, start:start + fresh, :].astype(mix_ref.dtype)
                    )

    policy()

    def multiply(buf, p, at):
        acc = jnp.dot(buf[0, at, :], wbuf[p, :dx, :], preferred_element_type=jnp.float32)
        for s in range(1, nt):
            acc = acc + jnp.dot(
                buf[s, at, :], wbuf[p, s * dx:(s + 1) * dx, :],
                preferred_element_type=jnp.float32,
            )
        return acc.astype(jnp.bfloat16)

    def project(p):
        @pl.when(jnp.logical_not(is_away(p) & at_end))
        def _():
            def take(d):
                o = jnp.where(d < z, d, d + 1)
                src = jnp.where(o < z, z - 1, z + 1)
                for r in range(SPLIT):
                    hop(src, z, lambda s: from_pair(p * SPLIT + r, o, s).wait_recv())

            each(0, nz - 1, take)
            row_tile = rows // 3

            def tile(r):
                at = pl.ds(pl.multiple_of(r * row_tile, row_tile), row_tile)
                acts[p, at, :] = multiply(xbuf, p, at)

            each(0, rows // row_tile, tile)

    def project_lent(i):
        def arrive(j):
            borrowed(j)[1]()

        each((i * nv + TILES - 1) // TILES, ((i + 1) * nv + TILES - 1) // TILES, arrive)
        at = tile_rows(i)

        def one(g):
            sres[g, at, :] = multiply(sbuf, 2 * g + 1, at)

        each(0, groups, one)

    def attend(p, i):
        away = p < 2 * groups
        late = p - 2 * groups
        g = jnp.where(away, p // 2, late // max(qchunks - 1, 1))
        j = jnp.where(away, qchunks - 1, lax.rem(late, max(qchunks - 1, 1)))
        head0 = (g * qchunks + j) * 2
        base = pl.multiple_of(g * CW, CW)
        b = i // per_cand
        start = (i - b * per_cand) * qrows
        at = tile_rows(i)
        new_at = pl.ds(pl.multiple_of(b * span, span), span)
        old_k = cbuf[b, :, pl.ds(base, HD)]
        old_v = cbuf[b, :, pl.ds(pl.multiple_of(base + HD, HD), HD)]
        new_k = acts[2 * g, new_at, :HD]
        new_v = acts[2 * g, new_at, HD:]
        q = jnp.concatenate([acts[p, at, :HD], acts[p, at, HD:]], axis=0)
        dims = (((1,), (1,)), ((), ()))
        s1 = lax.dot_general(q, old_k, dims, preferred_element_type=jnp.float32)
        s2 = lax.dot_general(q, new_k, dims, preferred_element_type=jnp.float32)
        ri = lax.broadcasted_iota(jnp.int32, s2.shape, 0)
        ci = lax.broadcasted_iota(jnp.int32, s2.shape, 1)
        ri = jnp.where(ri >= qrows, ri - qrows, ri) + start
        s2 = jnp.where(ri >= ci, s2, masked_value)
        top = jnp.maximum(jnp.max(s1, axis=1, keepdims=True), jnp.max(s2, axis=1, keepdims=True))
        scale = HD ** -0.5 * LOG2E
        e1 = jnp.exp2((s1 - top) * scale)
        e2 = jnp.exp2((s2 - top) * scale)
        total = jnp.sum(e1, axis=1, keepdims=True) + jnp.sum(e2, axis=1, keepdims=True)
        o = jnp.dot(e1.astype(jnp.bfloat16), old_v, preferred_element_type=jnp.float32)
        o = o + jnp.dot(e2.astype(jnp.bfloat16), new_v, preferred_element_type=jnp.float32)
        o = o / total
        part[b, pl.ds(pl.multiple_of(start, qrows), qrows), :] += (
            o[:qrows] * grade_ref[pl.ds(head0, 1), :]
            + o[qrows:] * grade_ref[pl.ds(head0 + 1, 1), :]
        )

    def count(steps, test):
        total = jnp.int32(0)
        for s in steps:
            total = total + test(s).astype(jnp.int32)
        return total

    def step(v, carry):
        ongoing = v < nv

        @pl.when(v + AHEAD < nv)
        def _():
            send_own(v + AHEAD)
            when(at_end, lambda: lend(v + AHEAD).start())

        when(ongoing, lambda: relay(v, 1, 2))

        @pl.when(v == 1)
        def _():
            others(lambda o: give(o).start())

        when(v == 3, collect)

        @pl.when(beside & ongoing & (v >= sx))
        def _():
            def start(j):
                lend(j).wait_recv()
                borrowed(j)[0]()

            each(jnp.where(v == sx, 0, v), v + 1, start)

        @pl.when(v == vx)
        def _():
            x_finish()
            c_load.wait()

        even = lax.rem(v, 2) == 0
        half = v // 2

        @pl.when(even & (v >= vx))
        def _():
            each(jnp.where(v == vx, 0, half - 1), half, project)

        when(ongoing, lambda: relay(v, 2, min(3, nz)))

        @pl.when(beside)
        def _():
            lo = count(sp_step, lambda s: s < v)
            hi = count(sp_step, lambda s: s <= v)
            each(lo, hi, project_lent)

        whole = jnp.logical_not(even) & (v >= vx + 1)
        first = jnp.where(v == vx + 1, 0, half - 1) * TILES
        ours = jnp.where(whole, half * TILES - first, 0)
        lo = count(off_step, lambda s: s < v)
        hi = count(off_step, lambda s: s <= v)
        theirs = jnp.where(at_end, (hi - lo) * groups, 0)

        def unit(n):
            mine_first = n < ours
            k = n - ours
            i_away = lo + k // groups
            g_away = k - (k // groups) * groups
            p = jnp.where(mine_first, (first + n) // TILES, 2 * g_away + 1)
            i = jnp.where(mine_first, lax.rem(first + n, TILES), i_away)
            when(jnp.logical_not(mine_first), lambda: get_back(g_away, i_away).wait_recv())

            @pl.when(jnp.logical_not(mine_first) | (is_query(p) & jnp.logical_not(is_away(p) & at_end)))
            def _():
                attend(p, i)

        each(0, ours + theirs, unit)

        when(ongoing, lambda: relay(v, 3, nz))

        @pl.when(beside)
        def _():
            lo = count(sp_step, lambda s: s < v)
            hi = count(sp_step, lambda s: s <= v)
            each(lo, hi, lambda i: each(0, groups, lambda g: give_back(g, i).start()))

        when(v >= LAG, lambda: drain(v - LAG))
        return carry

    lax.fori_loop(0, nv + 2, step, 0)

    for b in range(cands):
        toks[t, b:b + 1, :] = jnp.sum(part[b].T, axis=0, keepdims=True)
    each(nv + 2 - LAG, nv, drain)
    x_settle()

    def tell(o):
        return remote(toks.at[t], toks.at[t], t_send.at[o], t_recv.at[t], {"tensor": o})

    def hear(o):
        return remote(toks.at[o], toks.at[o], t_send.at[o], t_recv.at[o], {"tensor": o})

    each(1, nt, lambda d: tell(lax.rem(t + d, nt)).start())
    when(at_end, lambda: each(0, nv, lambda j: lend(j).wait_send()))

    @pl.when(beside)
    def _():
        each(0, nv, lambda j: borrowed(j)[2]())
        each(0, groups, lambda g: each(0, TILES, lambda i: give_back(g, i).wait_send()))

    def heard(d):
        o = lax.rem(t + d, nt)
        hear(o).wait_recv()
        tell(o).wait_send()

    each(1, nt, heard)
    total = toks[0]
    for o in range(1, nt):
        total = total + toks[o]
    reward_ref[...] = total


def local(
    nz, nt,
    response_latest_embeddings,
    critic_probe_projector,
    critic_pair_projector,
    critic_stored_pairs,
    critic_grading_vector,
    actor_stored_pairs,
    filled_extents,
    kept_responses,
    actor_latest_probes,
    actor_latest_pairs,
):
    cands, span, dx = response_latest_embeddings.shape
    rows = cands * span
    wq, wkv = critic_probe_projector, critic_pair_projector
    depth = wq.shape[0] * nz
    groups = wkv.shape[1] // CW
    per_group = wq.shape[1] // HD // groups
    nchunk = (wq.shape[1] + wkv.shape[1]) // CW
    nv = nchunk * SPLIT
    nx = nt // 2
    lanes, fresh, pwidth = actor_latest_probes.shape
    kv_here = actor_stored_pairs.shape[2]
    prows = pwidth // HD * fresh
    bf16, f32 = jnp.bfloat16, jnp.float32
    vmem = pl.BlockSpec(memory_space=pltpu.VMEM)
    smem = pl.BlockSpec(memory_space=pltpu.SMEM)
    anywhere = pl.BlockSpec(memory_space=pl.ANY)
    dma = pltpu.SemaphoreType.DMA
    token_rewards, mixed = pl.pallas_call(
        functools.partial(reward_kernel, nz, nt, per_group),
        out_shape=(
            jax.ShapeDtypeStruct((cands, span), f32),
            jax.ShapeDtypeStruct(actor_latest_probes.shape, bf16),
        ),
        in_specs=[anywhere] * 5 + [vmem] * 3 + [smem] * 2,
        out_specs=(vmem, vmem),
        scratch_shapes=[
            pltpu.VMEM((nt, rows, dx), bf16),
            pltpu.VMEM((nt, rows, dx), bf16),
            pltpu.VMEM((nchunk, depth, CW), bf16),
            pltpu.VMEM(critic_stored_pairs.shape, bf16),
            pltpu.VMEM(actor_stored_pairs.shape[1:], bf16),
            pltpu.VMEM((nchunk, rows, CW), bf16),
            pltpu.VMEM((groups, rows, CW), bf16),
            pltpu.VMEM((cands, span, HD), f32),
            pltpu.VMEM((nt, cands, span), f32),
            pltpu.VMEM((nz,) + actor_latest_probes.shape, bf16),
            pltpu.VMEM((nz,) + actor_latest_pairs.shape, bf16),
            pltpu.VMEM((cands, fresh, pwidth), f32),
            pltpu.VMEM((cands, fresh, actor_latest_pairs.shape[2]), f32),
            pltpu.VMEM((prows, HD), f32),
            pltpu.VMEM((kv_here * fresh, HD), f32),
            pltpu.VMEM((kv_here * fresh, HD), f32),
            pltpu.VMEM((nz, lanes, prows, HD), bf16),
            pltpu.VMEM((nz, lanes, prows, HD), bf16),
            pltpu.VMEM((lanes, prows, HD), f32),
            dma((nchunk + 2 + cands,)),
            dma((nv, nz)), dma((nv, nz)), dma((nv, nz)), dma((nv, nz)), dma((nv, nz)),
            dma((nx,)), dma((nx,)), dma((nx,)), dma((nx,)), dma((nx,)),
            dma((nv,)), dma((nv,)),
            dma((nv, nx)), dma((nv, nx)), dma((nv, nx)), dma((nv, nx)), dma((nv, nx)),
            dma((groups, TILES)), dma((groups, TILES)),
            dma((nt,)), dma((nt,)),
            dma((nz,)), dma((nz,)), dma((nz,)), dma((nz,)), dma((nz,)), dma((nz,)),
        ],
        compiler_params=pltpu.CompilerParams(
            collective_id=0, has_side_effects=True, vmem_limit_bytes=67043328
        ),
    )(
        response_latest_embeddings.reshape(rows, dx), wq, wkv, critic_stored_pairs,
        actor_stored_pairs, critic_grading_vector.reshape(-1, HD), actor_latest_probes,
        actor_latest_pairs, kept_responses, filled_extents,
    )
    return token_rewards, mixed


def solution(mesh):
    placed = (
        P(("groups", "cand"), None, "tensor"),
        P("cand", "tensor"),
        P("cand", "tensor"),
        P(("groups", "cand"), None, "tensor"),
        P("tensor"),
        P(("groups", "cand"), None, "tensor", None),
        P("groups"),
        P("groups"),
        P(("groups", "cand"), None, "tensor"),
        P(("groups", "cand"), None, "tensor"),
    )
    return jax.shard_map(
        functools.partial(local, mesh.shape["cand"], mesh.shape["tensor"]),
        mesh=mesh,
        in_specs=placed,
        out_specs=(P(("groups", "cand"), None), P(("groups", "cand"), None, "tensor")),
        check_vma=False,
    )
```

time: 285 us -> 268 us (0.940)
  blocking collectives: 6.24 us -> 0 us
  local copies, waits for them, and re-layouts: 7.83 us -> 2.54 us
  other arithmetic: 4.77 us -> 0 us
  Pallas kernels: 262 us -> 265 us
    psum x1 -> x0, blocking collectives: 6.24 us -> none  [local(): token_rewards = lax.psum(jnp.sum(shares, axis=-1), 'tensor')]
    slice x3 -> x0, local copies, waits for them, and re-layouts: 4.71 us -> none  [the longest x1 4.69 us: policy(): actor_stored_pairs[..., :HD]]
    pallas_call x2 -> x1, Pallas kernels: 262 us -> 265 us  [local(): pl.pallas_call(functools.partial(reward_kernel, nz, nt, per_group), out_s...]
where the time goes in v1:
time: 268 us
  Pallas kernels  265 us (99%)
    pallas_call x1, Pallas kernels, local(): pl.pallas_call(functools.partial(reward_kernel, nz, nt, per_group), out_s...  265 us

profile of v1, /device:TPU:0, one launch (start us, length us, event | category | flops | bytes accessed | tf_op | source)
XLA Modules:
  0.0 267.9 jit_solution(6650777818371475821)
XLA Ops:
  0.6 264.7 %shard_map.113 = (f32[2,384]{1,0:T(2,128)}, bf16[1,4,1024]{2,1,0:T(4,128)(2,1)}) custom-call(bf16[768,2048]{1,0:T(8,128)(2,1)} %bitcast.2, bf16[2048,1024]{1,0:T(8,128)(2,1)} %wq_ref.1, bf16[2048,512]{1,0:T(8,128)(2,1)} %wkv_ref.1, bf16[2,2048,512]{2,1,0:T(8,128)(2,1)} %cache_ref.1, bf16[2,2048,2,256]{3,2,1,0:T(2,128)(2,1)} %pcache_ref.1, f32[8,128]{1,0:T(8,128)} %bitcast.3, ...), custom_call_target="tpu_custom_call" | custom-call | tf_op jit(solution)/shard_map/pallas_call | solution.py:666
  265.4 1.2 copy.14
  266.6 1.3 copy.15

commit v2 on v1

--- a/solution.py
+++ b/solution.py
@@ -10,9 +10,16 @@
 HD = 128
 CW = 2 * HD
 SPLIT = 2
-AHEAD = 4
-LAG = 4
+AHEAD = 2
+LEAD = 1
+BEHIND = 2
+LAG = 2 * SPLIT
 TILES = 4
+BLOCKS = 3
+ROOM = 4.0
+KEYS = 512
+MIDDLE = 0.594
+COST = {"multiply": 1.3, "attend": 1.7, "lent": 1.0}
 MESH = pl.DeviceIdType.MESH
 
 masked_value = -1e30
@@ -21,6 +28,86 @@
 
 def when(cond, body):
     pl.when(cond)(body)
+
+
+def lookup(table, n):
+    value = jnp.int32(table[0])
+    for k in range(1, len(table)):
+        if table[k] != table[k - 1]:
+            value = jnp.where(n >= k, table[k], value)
+    return value
+
+
+def plan(nchunk, stride, cands):
+    nv = nchunk * SPLIT
+    groups = nchunk // stride
+    early = stride - 1
+    last = nchunk - 1
+    first_away = groups * early
+    x_step = [max(1, k * nv // 12) for k in (2, 4, 6)]
+    lent_step = [k * nv // 12 for k in (6, 8, 11)] + [nv]
+    per_cand = TILES // cands
+    todo_p = sorted(
+        (max(2 * SPLIT * (p + 1) + 2, 2 * x_step[r]), p, r)
+        for p in range(nchunk) for r in range(BLOCKS)
+    )
+    todo_p = [(min(w, 2 * nv + (p == last and r > 0)), p, r) for w, p, r in todo_p]
+    todo_s = sorted(
+        (max(min(2 * SPLIT * (first_away + g + 1) + 2, 2 * nv), 2 * lent_step[i]), i, g)
+        for g in range(groups) for i in range(TILES)
+    )
+    todo_a = [
+        (p, i) for p in range(nchunk) for i in range(TILES) if p >= first_away or p % early
+    ]
+    units = {"multiply": [], "attend": [], "lent": []}
+    ends = {k: [0] for k in units}
+    done = {}
+    lent_at = {}
+
+    def blocks(first, last):
+        return range(first * BLOCKS // TILES, -(-last * BLOCKS // TILES))
+
+    for w in range(2 * (nv + 2)):
+        left = ROOM if w < 2 * nv - 1 else 1e9
+        while todo_p and todo_p[0][0] <= w and left > 0:
+            _, p, r = todo_p.pop(0)
+            units["multiply"].append((p, r))
+            done[p, r] = w
+            left -= COST["multiply"]
+        while todo_s and todo_s[0][0] <= w and left > 0:
+            _, i, g = todo_s[0]
+            if (first_away + g, 0) not in done:
+                break
+            todo_s.pop(0)
+            units["lent"].append((g, i))
+            lent_at[g, i] = w // 2
+            left -= COST["lent"]
+        if w in (2 * nv - 1, 2 * nv):
+            left = 2 * COST["attend"] - 0.1 if w < 2 * nv else 0
+        while todo_a and left > 0:
+            ready = None
+            for p, i in todo_a:
+                b = i // per_cand
+                need = [(p, r) for r in blocks(i, i + 1)]
+                kv = p // early * early if p < first_away else (p - first_away) * early
+                need += [(kv, r) for r in blocks(b * per_cand, (b + 1) * per_cand)]
+                if all(n in done for n in need):
+                    ready = (p, i)
+                    break
+            if ready is None:
+                break
+            todo_a.remove(ready)
+            units["attend"].append(ready)
+            left -= COST["attend"]
+        for k in units:
+            ends[k].append(len(units[k]))
+    assert not (todo_p or todo_s or todo_a)
+    back = sorted(
+        (lent_at[u] + 2 if lent_at[u] + 2 <= nv else nv + 1, u[1], u[0]) for u in units["lent"]
+    )
+    units["back"] = [(g, i) for _, i, g in back]
+    ends["back"] = [sum(b[0] < v for b in back) for v in range(nv + 3)]
+    return units, ends, x_step
 
 
 def reward_kernel(
@@ -48,20 +135,19 @@
     groups = nchunk // (1 + qchunks)
     qrows = rows // TILES
     per_cand = TILES // cands
-    srows = rows // nv
-    vx = max(2, nv // 4 * 2)
-    sx = vx - 1
-    sp_step = []
-    for i in range(TILES):
-        at = nv if i == TILES - 1 else max(nv - TILES + 1 + i, 4 * groups + 1)
-        sp_step.append(at if at < nv else nv)
-    off_step = [s + 1 if s + 1 < nv else nv + 1 for s in sp_step]
+    lots = 2 * nchunk
+    per_lot = SPLIT // 2
+    srows = rows // lots
+    stride = 1 + qchunks
+    row_block = rows // BLOCKS
+    first_away = groups * qchunks
+    units, ends, x_step = plan(nchunk, stride, cands)
 
     def whole16(n):
         return max(sub // 2, int(round(n / 16)) * 16)
 
     share_first = whole16(sub * 2 / 3)
-    share_mid = whole16(sub * 7 / 12)
+    share_mid = whole16(sub * MIDDLE)
     share_last = sub // 2
 
     y = lax.axis_index("groups")
@@ -75,20 +161,19 @@
     outer = jnp.where(z == 1, 0, nz - 1)
 
     def is_away(p):
-        return (p < 2 * groups) & (lax.rem(p, 2) == 1)
-
-    def is_query(p):
-        return (p >= 2 * groups) | (lax.rem(p, 2) == 1)
+        return p >= first_away
+
+    def group_of(p):
+        return jnp.where(is_away(p), p - first_away, p // qchunks)
 
     def columns(p):
-        if p < 2 * groups:
-            g, j = p // 2, (p % 2) * qchunks
+        if p >= first_away:
+            g, j = p - first_away, qchunks - 1
         else:
-            g, j = divmod(p - 2 * groups, qchunks - 1)
-            j += 1
-        if j == 0:
+            g, j = p // qchunks, p % qchunks - 1
+        if j < 0:
             return wkv_ref.at[:, pl.ds(g * CW, CW)]
-        return wq_ref.at[:, pl.ds((g * qchunks + j - 1) * CW, CW)]
+        return wq_ref.at[:, pl.ds((g * qchunks + j) * CW, CW)]
 
     own_rows = pl.ds(pl.multiple_of(z * dz, dz), dz)
     loads = [
@@ -250,6 +335,7 @@
                     when(x > 0, lambda: to_left(x + d).start())
                     across(x + d, c).start()
 
+        def land():
             for o in range(nx):
                 across(o, 1 - c).wait_recv()
 
@@ -259,12 +345,14 @@
                 when((o <= x) & (x < nx - 1), lambda o=o: to_right(o).wait_send())
                 when((o >= x) & (x > 0), lambda o=o: to_left(o).wait_send())
 
-        return begin, finish, settle
-
-    x_begin, x_finish, x_settle = row_gather(
-        xbuf, pl.ds(0, rows), lambda o: x_right.at[o], lambda o: x_left.at[o],
-        lambda o: x_line.at[o], lambda o: x_psend.at[o], lambda o: x_precv.at[o],
-    )
+        return begin, finish, land, settle
+
+    def own_block(r):
+        return row_gather(
+            xbuf, pl.ds(pl.multiple_of(r * row_block, row_block), row_block),
+            lambda o: x_right.at[r, o], lambda o: x_left.at[r, o], lambda o: x_line.at[r, o],
+            lambda o: x_psend.at[r, o], lambda o: x_precv.at[r, o],
+        )
 
     def span_rows(j):
         return pl.ds(pl.multiple_of(j * srows, srows), srows)
@@ -287,12 +375,12 @@
     def give_back(g, i):
         at = tile_rows(i)
         return remote(
-            sres.at[g, at, :], acts.at[2 * g + 1, at, :], r_send.at[g, i], r_recv.at[g, i],
+            sres.at[g, at, :], acts.at[first_away + g, at, :], r_send.at[g, i], r_recv.at[g, i],
             {"cand": outer},
         )
 
     def get_back(g, i):
-        at = acts.at[2 * g + 1, tile_rows(i), :]
+        at = acts.at[first_away + g, tile_rows(i), :]
         return remote(at, at, r_send.at[g, i], r_recv.at[g, i], {"cand": inner})
 
     def each(first, last, body):
@@ -317,12 +405,22 @@
         if v % SPLIT == 0:
             loads[v // SPLIT].wait()
         send_own(v)
-        if v == 0:
-            x_load.wait()
-            x_begin()
-        when(at_end, lambda v=v: lend(v).start())
+    x_load.wait()
+    for r in range(BLOCKS):
+        own_block(r)[0]()
     for p in range(-(-AHEAD // SPLIT), nchunk):
         loads[p].wait()
+
+    @pl.when(at_end)
+    def _():
+        def queue(v):
+            send_own(v)
+            j = v // per_lot - BEHIND
+            when((lax.rem(v, per_lot) == per_lot - 1) & (j >= 0), lambda: lend(j).start())
+
+        each(AHEAD, nv, queue)
+        each(lots - BEHIND, lots, lambda j: lend(j).start())
+
     part[...] = jnp.zeros_like(part)
 
     lanes, fresh, _ = probes_ref.shape
@@ -451,151 +549,174 @@
             )
         return acc.astype(jnp.bfloat16)
 
-    def project(p):
+    def project(n):
+        p = lookup([u[0] for u in units["multiply"]], n)
+        r = lookup([u[1] for u in units["multiply"]], n)
+
         @pl.when(jnp.logical_not(is_away(p) & at_end))
         def _():
             def take(d):
                 o = jnp.where(d < z, d, d + 1)
                 src = jnp.where(o < z, z - 1, z + 1)
-                for r in range(SPLIT):
-                    hop(src, z, lambda s: from_pair(p * SPLIT + r, o, s).wait_recv())
-
-            each(0, nz - 1, take)
-            row_tile = rows // 3
-
-            def tile(r):
-                at = pl.ds(pl.multiple_of(r * row_tile, row_tile), row_tile)
-                acts[p, at, :] = multiply(xbuf, p, at)
-
-            each(0, rows // row_tile, tile)
-
-    def project_lent(i):
-        def arrive(j):
-            borrowed(j)[1]()
-
-        each((i * nv + TILES - 1) // TILES, ((i + 1) * nv + TILES - 1) // TILES, arrive)
+                for q in range(SPLIT):
+                    hop(src, z, lambda s: from_pair(p * SPLIT + q, o, s).wait_recv())
+
+            when(r == 0, lambda: each(0, nz - 1, take))
+            at = pl.ds(pl.multiple_of(r * row_block, row_block), row_block)
+            acts[p, at, :] = multiply(xbuf, p, at)
+
+    def lent_unit(n):
+        g = lookup([u[0] for u in units["lent"]], n)
+        i = lookup([u[1] for u in units["lent"]], n)
+        return g, i
+
+    def project_lent(n):
+        g, i = lent_unit(n)
+
+        @pl.when(g == 0)
+        def _():
+            first = (i * lots + TILES - 1) // TILES
+            last = ((i + 1) * lots + TILES - 1) // TILES
+            @pl.when(i == TILES - 1)
+            def _():
+                borrowed(lots - 2)[1]()
+                borrowed(lots - 1)[1]()
+
+            each(first, last, lambda j: borrowed(j)[2]())
+
         at = tile_rows(i)
-
-        def one(g):
-            sres[g, at, :] = multiply(sbuf, 2 * g + 1, at)
-
-        each(0, groups, one)
+        sres[g, at, :] = multiply(sbuf, first_away + g, at)
 
     def attend(p, i):
-        away = p < 2 * groups
-        late = p - 2 * groups
-        g = jnp.where(away, p // 2, late // max(qchunks - 1, 1))
-        j = jnp.where(away, qchunks - 1, lax.rem(late, max(qchunks - 1, 1)))
+        g = group_of(p)
+        j = jnp.where(is_away(p), qchunks - 1, lax.rem(p, qchunks) - 1)
         head0 = (g * qchunks + j) * 2
         base = pl.multiple_of(g * CW, CW)
         b = i // per_cand
         start = (i - b * per_cand) * qrows
         at = tile_rows(i)
         new_at = pl.ds(pl.multiple_of(b * span, span), span)
-        old_k = cbuf[b, :, pl.ds(base, HD)]
-        old_v = cbuf[b, :, pl.ds(pl.multiple_of(base + HD, HD), HD)]
-        new_k = acts[2 * g, new_at, :HD]
-        new_v = acts[2 * g, new_at, HD:]
         q = jnp.concatenate([acts[p, at, :HD], acts[p, at, HD:]], axis=0)
         dims = (((1,), (1,)), ((), ()))
-        s1 = lax.dot_general(q, old_k, dims, preferred_element_type=jnp.float32)
-        s2 = lax.dot_general(q, new_k, dims, preferred_element_type=jnp.float32)
-        ri = lax.broadcasted_iota(jnp.int32, s2.shape, 0)
-        ci = lax.broadcasted_iota(jnp.int32, s2.shape, 1)
+        scale = HD ** -0.5 * LOG2E
+
+        def scores(keys):
+            return lax.dot_general(q, keys, dims, preferred_element_type=jnp.float32)
+
+        def weigh(e, values):
+            both = jnp.concatenate([values, jnp.ones_like(values)], axis=1)
+            return jnp.dot(e.astype(jnp.bfloat16), both, preferred_element_type=jnp.float32)
+
+        s = scores(acts[g * qchunks, new_at, :HD])
+        ri = lax.broadcasted_iota(jnp.int32, s.shape, 0)
+        ci = lax.broadcasted_iota(jnp.int32, s.shape, 1)
         ri = jnp.where(ri >= qrows, ri - qrows, ri) + start
-        s2 = jnp.where(ri >= ci, s2, masked_value)
-        top = jnp.maximum(jnp.max(s1, axis=1, keepdims=True), jnp.max(s2, axis=1, keepdims=True))
-        scale = HD ** -0.5 * LOG2E
-        e1 = jnp.exp2((s1 - top) * scale)
-        e2 = jnp.exp2((s2 - top) * scale)
-        total = jnp.sum(e1, axis=1, keepdims=True) + jnp.sum(e2, axis=1, keepdims=True)
-        o = jnp.dot(e1.astype(jnp.bfloat16), old_v, preferred_element_type=jnp.float32)
-        o = o + jnp.dot(e2.astype(jnp.bfloat16), new_v, preferred_element_type=jnp.float32)
-        o = o / total
+        s = jnp.where(ri >= ci, s, masked_value)
+        top = jnp.max(s, axis=1, keepdims=True)
+        o = weigh(jnp.exp2((s - top) * scale), acts[g * qchunks, new_at, HD:])
+        for first in range(0, cbuf.shape[1], KEYS):
+            keys = pl.ds(first, min(KEYS, cbuf.shape[1] - first))
+            s = scores(cbuf[b, keys, pl.ds(base, HD)])
+            higher = jnp.maximum(top, jnp.max(s, axis=1, keepdims=True))
+            o = o * jnp.exp2((top - higher) * scale)
+            top = higher
+            o = o + weigh(
+                jnp.exp2((s - top) * scale), cbuf[b, keys, pl.ds(pl.multiple_of(base + HD, HD), HD)]
+            )
+        o = o[:, :HD] / o[:, HD:]
         part[b, pl.ds(pl.multiple_of(start, qrows), qrows), :] += (
             o[:qrows] * grade_ref[pl.ds(head0, 1), :]
             + o[qrows:] * grade_ref[pl.ds(head0 + 1, 1), :]
         )
 
-    def count(steps, test):
-        total = jnp.int32(0)
-        for s in steps:
-            total = total + test(s).astype(jnp.int32)
-        return total
+    def take_lot(j):
+        lend(j).wait_recv()
+        borrowed(j)[0]()
+        when((j > 0) & (j < lots - 1), lambda: borrowed(j - 1)[1]())
+
+    def compute(v, half):
+        w = 2 * v + half
+        when(beside & (w == 2 * nv - 1), lambda: take_lot(lots - 2))
+
+        def between(kind):
+            return lookup(ends[kind], w), lookup(ends[kind], w + 1)
+
+        @pl.when(beside & (w > 0))
+        def _():
+            def send_back(n):
+                g, i = lent_unit(n)
+                give_back(g, i).start()
+
+            each(lookup(ends["lent"], w - 1), lookup(ends["lent"], w), send_back)
+
+        each(*between("multiply"), project)
+
+        @pl.when(beside)
+        def _():
+            each(*between("lent"), project_lent)
+
+        when(beside & (w == 2 * nv - 1), lambda: take_lot(lots - 1))
+        a_lo, a_hi = between("attend")
+        b_lo, b_hi = lookup(ends["back"], v), lookup(ends["back"], v + 1)
+        ours = a_hi - a_lo
+        theirs = jnp.where(at_end & (half == 0), b_hi - b_lo, 0)
+
+        def unit(n):
+            own = n < ours
+            k = b_lo + n - ours
+            g_back = lookup([u[0] for u in units["back"]], k)
+            i_back = lookup([u[1] for u in units["back"]], k)
+            p_own = lookup([u[0] for u in units["attend"]], a_lo + n)
+            i_own = lookup([u[1] for u in units["attend"]], a_lo + n)
+            p = jnp.where(own, p_own, first_away + g_back)
+            i = jnp.where(own, i_own, i_back)
+            when(jnp.logical_not(own), lambda: get_back(g_back, i_back).wait_recv())
+
+            @pl.when(jnp.logical_not(own & is_away(p) & at_end))
+            def _():
+                attend(p, i)
+
+        each(0, ours + theirs, unit)
 
     def step(v, carry):
         ongoing = v < nv
 
-        @pl.when(v + AHEAD < nv)
+        each(
+            jnp.where(v == 0, 0, v + LEAD), jnp.minimum(v + LEAD + 1, nv), lambda u: relay(u, 1, 2)
+        )
+
+        @pl.when((v + AHEAD < nv) & jnp.logical_not(at_end))
         def _():
             send_own(v + AHEAD)
-            when(at_end, lambda: lend(v + AHEAD).start())
-
-        when(ongoing, lambda: relay(v, 1, 2))
 
         @pl.when(v == 1)
         def _():
             others(lambda o: give(o).start())
 
-        when(v == 3, collect)
-
-        @pl.when(beside & ongoing & (v >= sx))
-        def _():
-            def start(j):
-                lend(j).wait_recv()
-                borrowed(j)[0]()
-
-            each(jnp.where(v == sx, 0, v), v + 1, start)
-
-        @pl.when(v == vx)
-        def _():
-            x_finish()
-            c_load.wait()
-
-        even = lax.rem(v, 2) == 0
-        half = v // 2
-
-        @pl.when(even & (v >= vx))
-        def _():
-            each(jnp.where(v == vx, 0, half - 1), half, project)
-
-        when(ongoing, lambda: relay(v, 2, min(3, nz)))
-
-        @pl.when(beside)
-        def _():
-            lo = count(sp_step, lambda s: s < v)
-            hi = count(sp_step, lambda s: s <= v)
-            each(lo, hi, project_lent)
-
-        whole = jnp.logical_not(even) & (v >= vx + 1)
-        first = jnp.where(v == vx + 1, 0, half - 1) * TILES
-        ours = jnp.where(whole, half * TILES - first, 0)
-        lo = count(off_step, lambda s: s < v)
-        hi = count(off_step, lambda s: s <= v)
-        theirs = jnp.where(at_end, (hi - lo) * groups, 0)
-
-        def unit(n):
-            mine_first = n < ours
-            k = n - ours
-            i_away = lo + k // groups
-            g_away = k - (k // groups) * groups
-            p = jnp.where(mine_first, (first + n) // TILES, 2 * g_away + 1)
-            i = jnp.where(mine_first, lax.rem(first + n, TILES), i_away)
-            when(jnp.logical_not(mine_first), lambda: get_back(g_away, i_away).wait_recv())
-
-            @pl.when(jnp.logical_not(mine_first) | (is_query(p) & jnp.logical_not(is_away(p) & at_end)))
+        when(v == nv + 1, collect)
+
+        for r in range(BLOCKS):
+            @pl.when(v == x_step[r])
+            def _(r=r):
+                own_block(r)[1]()
+                own_block(r)[2]()
+
+        when(v == x_step[0], c_load.wait)
+
+        def rest(half, carry):
+            compute(v, half)
+            j = v // per_lot - BEHIND
+            due = ongoing & (half == 0) & (lax.rem(v, per_lot) == per_lot - 1) & (j >= 0)
+            when(beside & due, lambda: take_lot(j))
+
+            @pl.when(ongoing & (half == 0))
             def _():
-                attend(p, i)
-
-        each(0, ours + theirs, unit)
-
+                relay(v, 2, min(3, nz))
+
+            return carry
+
+        lax.fori_loop(0, 2, rest, 0)
         when(ongoing, lambda: relay(v, 3, nz))
-
-        @pl.when(beside)
-        def _():
-            lo = count(sp_step, lambda s: s < v)
-            hi = count(sp_step, lambda s: s <= v)
-            each(lo, hi, lambda i: each(0, groups, lambda g: give_back(g, i).start()))
 
         when(v >= LAG, lambda: drain(v - LAG))
         return carry
@@ -605,7 +726,8 @@
     for b in range(cands):
         toks[t, b:b + 1, :] = jnp.sum(part[b].T, axis=0, keepdims=True)
     each(nv + 2 - LAG, nv, drain)
-    x_settle()
+    for r in range(BLOCKS):
+        own_block(r)[3]()
 
     def tell(o):
         return remote(toks.at[t], toks.at[t], t_send.at[o], t_recv.at[t], {"tensor": o})
@@ -614,11 +736,11 @@
         return remote(toks.at[o], toks.at[o], t_send.at[o], t_recv.at[o], {"tensor": o})
 
     each(1, nt, lambda d: tell(lax.rem(t + d, nt)).start())
-    when(at_end, lambda: each(0, nv, lambda j: lend(j).wait_send()))
+    when(at_end, lambda: each(0, lots, lambda j: lend(j).wait_send()))
 
     @pl.when(beside)
     def _():
-        each(0, nv, lambda j: borrowed(j)[2]())
+        each(0, lots, lambda j: borrowed(j)[3]())
         each(0, groups, lambda g: each(0, TILES, lambda i: give_back(g, i).wait_send()))
 
     def heard(d):
@@ -654,6 +776,7 @@
     per_group = wq.shape[1] // HD // groups
     nchunk = (wq.shape[1] + wkv.shape[1]) // CW
     nv = nchunk * SPLIT
+    lots = 2 * nchunk
     nx = nt // 2
     lanes, fresh, pwidth = actor_latest_probes.shape
     kv_here = actor_stored_pairs.shape[2]
@@ -693,9 +816,9 @@
             pltpu.VMEM((lanes, prows, HD), f32),
             dma((nchunk + 2 + cands,)),
             dma((nv, nz)), dma((nv, nz)), dma((nv, nz)), dma((nv, nz)), dma((nv, nz)),
-            dma((nx,)), dma((nx,)), dma((nx,)), dma((nx,)), dma((nx,)),
-            dma((nv,)), dma((nv,)),
-            dma((nv, nx)), dma((nv, nx)), dma((nv, nx)), dma((nv, nx)), dma((nv, nx)),
+            dma((BLOCKS, nx)), dma((BLOCKS, nx)), dma((BLOCKS, nx)), dma((BLOCKS, nx)), dma((BLOCKS, nx)),
+            dma((lots,)), dma((lots,)),
+            dma((lots, nx)), dma((lots, nx)), dma((lots, nx)), dma((lots, nx)), dma((lots, nx)),
             dma((groups, TILES)), dma((groups, TILES)),
             dma((nt,)), dma((nt,)),
             dma((nz,)), dma((nz,)), dma((nz,)), dma((nz,)), dma((nz,)), dma((nz,)),

time: 268 us -> 219 us (0.82)
  Pallas kernels: 265 us -> 215 us
    pallas_call x1, Pallas kernels: 265 us -> 215 us  [local(): pl.pallas_call(functools.partial(reward_kernel, nz, nt, per_group), out_s...]
where the time goes in v2:
time: 219 us
  Pallas kernels  215 us (98%)
  local copies, waits for them, and re-layouts  2.54 us (1%)
    pallas_call x1, Pallas kernels, local(): pl.pallas_call(functools.partial(reward_kernel, nz, nt, per_group), out_s...  215 us

profile of v2, /device:TPU:0, one launch (start us, length us, event | category | flops | bytes accessed | tf_op | source)
XLA Modules:
  0.0 218.6 jit_solution(3258314579570541803)
XLA Ops:
  0.6 215.4 %shard_map.113 = (f32[2,384]{1,0:T(2,128)}, bf16[1,4,1024]{2,1,0:T(4,128)(2,1)}) custom-call(bf16[768,2048]{1,0:T(8,128)(2,1)} %bitcast.2, bf16[2048,1024]{1,0:T(8,128)(2,1)} %wq_ref.1, bf16[2048,512]{1,0:T(8,128)(2,1)} %wkv_ref.1, bf16[2,2048,512]{2,1,0:T(8,128)(2,1)} %cache_ref.1, bf16[2,2048,2,256]{3,2,1,0:T(2,128)(2,1)} %pcache_ref.1, f32[8,128]{1,0:T(8,128)} %bitcast.3, ...), custom_call_target="tpu_custom_call" | custom-call | tf_op jit(solution)/shard_map/pallas_call | solution.py:789
  216.0 1.2 copy.14
  217.3 1.3 copy.15

commit v3 on v2

--- a/solution.py
+++ b/solution.py
@@ -45,7 +45,7 @@
     last = nchunk - 1
     first_away = groups * early
     x_step = [max(1, k * nv // 12) for k in (2, 4, 6)]
-    lent_step = [k * nv // 12 for k in (6, 8, 11)] + [nv]
+    lent_step = [k * nv // 12 for k in (6, 8, 11)] + [nv + 1]
     per_cand = TILES // cands
     todo_p = sorted(
         (max(2 * SPLIT * (p + 1) + 2, 2 * x_step[r]), p, r)
@@ -82,8 +82,9 @@
             units["lent"].append((g, i))
             lent_at[g, i] = w // 2
             left -= COST["lent"]
-        if w in (2 * nv - 1, 2 * nv):
-            left = 2 * COST["attend"] - 0.1 if w < 2 * nv else 0
+        if w >= 2 * nv - 1:
+            left = 99 if w in (2 * nv - 1, 2 * nv + 3) else 0
+            left = left * COST["attend"] - 0.1
         while todo_a and left > 0:
             ready = None
             for p, i in todo_a:
@@ -103,9 +104,9 @@
             ends[k].append(len(units[k]))
     assert not (todo_p or todo_s or todo_a)
     back = sorted(
-        (lent_at[u] + 2 if lent_at[u] + 2 <= nv else nv + 1, u[1], u[0]) for u in units["lent"]
+        (lent_at[u] + 2 if lent_at[u] + 2 <= nv else nv + 1, lent_at[u], u[1], u[0]) for u in units["lent"]
     )
-    units["back"] = [(g, i) for _, i, g in back]
+    units["back"] = [(g, i) for _, _, i, g in back]
     ends["back"] = [sum(b[0] < v for b in back) for v in range(nv + 3)]
     return units, ends, x_step
 
@@ -636,7 +637,7 @@
 
     def compute(v, half):
         w = 2 * v + half
-        when(beside & (w == 2 * nv - 1), lambda: take_lot(lots - 2))
+        when(beside & (w == 2 * nv), lambda: take_lot(lots - 1))
 
         def between(kind):
             return lookup(ends[kind], w), lookup(ends[kind], w + 1)
@@ -655,7 +656,7 @@
         def _():
             each(*between("lent"), project_lent)
 
-        when(beside & (w == 2 * nv - 1), lambda: take_lot(lots - 1))
+        when(beside & (w == 2 * nv - 1), lambda: take_lot(lots - 2))
         a_lo, a_hi = between("attend")
         b_lo, b_hi = lookup(ends["back"], v), lookup(ends["back"], v + 1)
         ours = a_hi - a_lo

time: 219 us -> 215 us (0.982)
  Pallas kernels: 215 us -> 211 us
    pallas_call x1, Pallas kernels: 215 us -> 211 us  [local(): pl.pallas_call(functools.partial(reward_kernel, nz, nt, per_group), out_s...]
where the time goes in v3:
time: 215 us; the launch traced here: 214 us
  Pallas kernels  211 us (98%)
  local copies, waits for them, and re-layouts  2.54 us (1%)
    pallas_call x1, Pallas kernels, local(): pl.pallas_call(functools.partial(reward_kernel, nz, nt, per_group), out_s...  211 us

profile of v3, /device:TPU:0, one launch (start us, length us, event | category | flops | bytes accessed | tf_op | source)
XLA Modules:
  0.0 214.5 jit_solution(8851211461103950733)
XLA Ops:
  0.6 211.3 %shard_map.113 = (f32[2,384]{1,0:T(2,128)}, bf16[1,4,1024]{2,1,0:T(4,128)(2,1)}) custom-call(bf16[768,2048]{1,0:T(8,128)(2,1)} %bitcast.2, bf16[2048,1024]{1,0:T(8,128)(2,1)} %wq_ref.1, bf16[2048,512]{1,0:T(8,128)(2,1)} %wkv_ref.1, bf16[2,2048,512]{2,1,0:T(8,128)(2,1)} %cache_ref.1, bf16[2,2048,2,256]{3,2,1,0:T(2,128)(2,1)} %pcache_ref.1, f32[8,128]{1,0:T(8,128)} %bitcast.3, ...), custom_call_target="tpu_custom_call" | custom-call | tf_op jit(solution)/shard_map/pallas_call | solution.py:790
  211.9 1.2 copy.14
  213.2 1.3 copy.15

commit v4 on v3

--- a/solution.py
+++ b/solution.py
@@ -14,10 +14,11 @@
 LEAD = 1
 BEHIND = 2
 LAG = 2 * SPLIT
+WINDOW = LEAD + LAG + 1
 TILES = 4
 BLOCKS = 3
 ROOM = 4.0
-KEYS = 512
+KEYS = 256
 MIDDLE = 0.594
 COST = {"multiply": 1.3, "attend": 1.7, "lent": 1.0}
 MESH = pl.DeviceIdType.MESH
@@ -118,9 +119,9 @@
     reward_ref, mix_ref,
     xbuf, sbuf, wbuf, cbuf, pbuf, acts, sres, part, toks,
     qall, pall, qsel, psel, qrow, krow, vrow, placed, given, mine,
-    load_sem, right_sem, left_sem, line_sem, pair_send, pair_recv,
-    x_right, x_left, x_line, x_psend, x_precv,
-    s_send, s_recv, sx_right, sx_left, sx_line, sx_psend, sx_precv,
+    load_sem, hop_sem, line_sem, pair_send, pair_recv,
+    x_hop, x_line, x_psend, x_precv,
+    s_recv, sx_hop, sx_line, sx_psend, sx_precv,
     r_send, r_recv, t_send, t_recv,
     q_send, q_recv, p_send, p_recv, give_send, give_recv,
 ):
@@ -233,19 +234,19 @@
 
     def go_right(v, o, s):
         ref = piece(v, o, y * (sub - s), s)
-        return remote(ref, ref, right_sem.at[v, o], line_sem.at[v, o], {"cand": z + 1})
+        return remote(ref, ref, hop_sem.at[v, o], line_sem.at[v, o], {"cand": z + 1})
 
     def go_left(v, o, s):
         ref = piece(v, o, y * (sub - s), s)
-        return remote(ref, ref, left_sem.at[v, o], line_sem.at[v, o], {"cand": z - 1})
+        return remote(ref, ref, hop_sem.at[v, o + 1], line_sem.at[v, o], {"cand": z - 1})
 
     def to_pair(v, o, s):
         ref = piece(v, o, y * s, sub - s)
-        return remote(ref, ref, pair_send.at[v, o], pair_recv.at[v, o], {"groups": 1 - y})
+        return remote(ref, ref, pair_send.at[lax.rem(v, WINDOW), o], pair_recv.at[v, o], {"groups": 1 - y})
 
     def from_pair(v, o, s):
         ref = piece(v, o, (1 - y) * s, sub - s)
-        return remote(ref, ref, pair_send.at[v, o], pair_recv.at[v, o], {"groups": 1 - y})
+        return remote(ref, ref, pair_send.at[lax.rem(v, WINDOW), o], pair_recv.at[v, o], {"groups": 1 - y})
 
     def sends_right(p):
         return (z < nz - 1) & jnp.logical_not(is_away(p) & (z + 1 == nz - 1))
@@ -351,7 +352,7 @@
     def own_block(r):
         return row_gather(
             xbuf, pl.ds(pl.multiple_of(r * row_block, row_block), row_block),
-            lambda o: x_right.at[r, o], lambda o: x_left.at[r, o], lambda o: x_line.at[r, o],
+            lambda o: x_hop.at[r, o], lambda o: x_hop.at[r, o + 1], lambda o: x_line.at[r, o],
             lambda o: x_psend.at[r, o], lambda o: x_precv.at[r, o],
         )
 
@@ -361,12 +362,12 @@
     def lend(j):
         at = span_rows(j)
         return remote(
-            xbuf.at[t, at, :], sbuf.at[t, at, :], s_send.at[j], s_recv.at[j], {"cand": inner}
+            xbuf.at[t, at, :], sbuf.at[t, at, :], sx_psend.at[j, 0], s_recv.at[j], {"cand": inner}
         )
 
     def borrowed(j):
         return row_gather(
-            sbuf, span_rows(j), lambda o: sx_right.at[j, o], lambda o: sx_left.at[j, o],
+            sbuf, span_rows(j), lambda o: sx_hop.at[j, o], lambda o: sx_hop.at[j, o + 1],
             lambda o: sx_line.at[j, o], lambda o: sx_psend.at[j, o], lambda o: sx_precv.at[j, o],
         )
 
@@ -816,10 +817,10 @@
             pltpu.VMEM((nz, lanes, prows, HD), bf16),
             pltpu.VMEM((lanes, prows, HD), f32),
             dma((nchunk + 2 + cands,)),
-            dma((nv, nz)), dma((nv, nz)), dma((nv, nz)), dma((nv, nz)), dma((nv, nz)),
-            dma((BLOCKS, nx)), dma((BLOCKS, nx)), dma((BLOCKS, nx)), dma((BLOCKS, nx)), dma((BLOCKS, nx)),
-            dma((lots,)), dma((lots,)),
-            dma((lots, nx)), dma((lots, nx)), dma((lots, nx)), dma((lots, nx)), dma((lots, nx)),
+            dma((nv, nz + 1)), dma((nv, nz)), dma((WINDOW, nz)), dma((nv, nz)),
+            dma((BLOCKS, nx + 1)), dma((BLOCKS, nx)), dma((BLOCKS, nx)), dma((BLOCKS, nx)),
+            dma((lots,)),
+            dma((lots, nx + 1)), dma((lots, nx)), dma((lots, nx)), dma((lots, nx)),
             dma((groups, TILES)), dma((groups, TILES)),
             dma((nt,)), dma((nt,)),
             dma((nz,)), dma((nz,)), dma((nz,)), dma((nz,)), dma((nz,)), dma((nz,)),

time: 215 us -> 214 us (level)
  no operation moved by 1% of the time
where the time goes in v4:
time: 214 us; the launch traced here: 213 us
  Pallas kernels  210 us (98%)
  local copies, waits for them, and re-layouts  2.54 us (1%)
    pallas_call x1, Pallas kernels, local(): pl.pallas_call(functools.partial(reward_kernel, nz, nt, per_group), out_s...  210 us

profile of v4, /device:TPU:0, one launch (start us, length us, event | category | flops | bytes accessed | tf_op | source)
XLA Modules:
  0.0 213.4 jit_solution(1522331031834514661)
XLA Ops:
  0.6 210.3 %shard_map.113 = (f32[2,384]{1,0:T(2,128)}, bf16[1,4,1024]{2,1,0:T(4,128)(2,1)}) custom-call(bf16[768,2048]{1,0:T(8,128)(2,1)} %bitcast.2, bf16[2048,1024]{1,0:T(8,128)(2,1)} %wq_ref.1, bf16[2048,512]{1,0:T(8,128)(2,1)} %wkv_ref.1, bf16[2,2048,512]{2,1,0:T(8,128)(2,1)} %cache_ref.1, bf16[2,2048,2,256]{3,2,1,0:T(2,128)(2,1)} %pcache_ref.1, f32[8,128]{1,0:T(8,128)} %bitcast.3, ...), custom_call_target="tpu_custom_call" | custom-call | tf_op jit(solution)/shard_map/pallas_call | solution.py:791
  210.9 1.2 copy.14
  212.1 1.3 copy.15
